TPU v7x, 32 devices: a whole 2x2x4 slice. The times are simulated.
32 devices in a mesh: dp: 4 (over y, core), tensor: 8 (over z, x).
Axes of the slice: x: 2, y: 2, z: 4, core: 2. Of those that a mesh axis runs over, the one named last changes fastest.
Arguments:
- block_input: float32 [4, 2048, 1024], P('dp', 'tensor'), may hold values from -6 to 6
- segment_ids: int32 [4, 2048], P('dp'), may hold values from 0 to 2, as said below
- positions: int32 [4, 2048], P('dp'), may hold values from 0 to 1791, as said below
- attention_gain: bfloat16 [1024], P('dp'), may hold values from 0.099609375 to 1.8984375
- feedforward_gain: bfloat16 [1024], P('dp'), may hold values from 0.099609375 to 1.8984375
- qkv_weight: bfloat16 [1024, 3, 1024], P('dp', None, 'tensor'), may hold values from -2 to 2, as said below
- output_weight: bfloat16 [1024, 1024], P('tensor', 'dp'), may hold values from -0.75 to 0.75
- expand_weight: bfloat16 [1024, 2, 2624], P('dp', None, 'tensor'), may hold values from -0.1875 to 0.1875
- contract_weight: bfloat16 [2624, 1024], P('tensor', 'dp'), may hold values from -0.25 to 0.25
- cotangent: float32 [4, 2048, 1024], P('dp', 'tensor'), may hold values from -6 to 6
Outputs:
- block_output: float32 [4, 2048, 1024], P('dp', 'tensor')
- input_grad: float32 [4, 2048, 1024], P('dp', 'tensor')
- attention_gain_grad: float32 [1024], P('dp')
- feedforward_gain_grad: float32 [1024], P('dp')
- qkv_grad: float32 [1024, 3, 1024], P('dp', None, 'tensor')
- output_grad: float32 [1024, 1024], P('tensor', 'dp')
- expand_grad: float32 [1024, 2, 2624], P('dp', None, 'tensor')
- contract_grad: float32 [2624, 1024], P('tensor', 'dp')
Inputs may be any that keep to these rules, and one draw needn't show every extreme that they name: `segment_ids`: within each sequence the numbers never fall; a token's number tells its document, and a number may be skipped. `positions`: each token's position counts the tokens before it in its own document; no document is longer than 1792 tokens, and some document is that long. `qkv_weight`: the joined query, key and value projection.
All inputs are finite; a program needn't handle non-finite values.
Results may differ from a plain program's by a relative error of at most 0.025.
Values may be sent and summed in bfloat16 or wider, within the bound.
A program may use at most 128 MiB of HBM per device.

v0:
```python
import math
import jax
import jax.numpy as jnp
from jax import lax
from jax.sharding import PartitionSpec as P

HD = 64
WINDOW = 128
EPSILON = 1e-05
MASKED = -1e30
ROOT_HALF = 0.7071067811865476
DENSITY = 0.3989422804014327


def layer_norm(values, gain_vector):
    centre = values - jnp.mean(values, axis=-1, keepdims=True)
    variance = jnp.mean(centre * centre, axis=-1, keepdims=True)
    inverse = lax.rsqrt(variance + EPSILON)
    normed = centre * inverse
    return (normed, inverse, (normed * gain_vector.astype(jnp.float32)).astype(jnp.bfloat16))


def norm_backward(upstream, normed, inverse, gain_vector):
    scaled = upstream * gain_vector.astype(jnp.float32)
    inner_term = (
        scaled
        - jnp.mean(scaled, axis=-1, keepdims=True)
        - normed * jnp.mean(scaled * normed, axis=-1, keepdims=True)
    )
    return (inverse * inner_term, jnp.sum(upstream * normed, axis=0))


def gelu_pair(values):
    normal_cdf = 0.5 * (1.0 + lax.erf(values * ROOT_HALF))
    return (values * normal_cdf, normal_cdf + values * DENSITY * jnp.exp(-0.5 * values * values))


def rope_tables(places, head_size):
    half_size = head_size // 2
    frequency = jnp.exp(
        jnp.arange(half_size, dtype=jnp.float32) * (-2.0 * math.log(10000.0) / head_size)
    )
    angles = places.astype(jnp.float32)[:, None] * frequency[None, :]
    cosine_table = jnp.concatenate([jnp.cos(angles), jnp.cos(angles)], axis=-1)[:, None, :]
    sine_table = jnp.concatenate([jnp.sin(angles), jnp.sin(angles)], axis=-1)[:, None, :]
    return (cosine_table, sine_table)


def rotate(tensor, cosine_table, sine_table):
    half_size = tensor.shape[-1] // 2
    turned = jnp.concatenate([-tensor[..., half_size:], tensor[..., :half_size]], axis=-1)
    return tensor * cosine_table + turned * sine_table


def unrotate(tensor, cosine_table, sine_table):
    half_size = tensor.shape[-1] // 2
    weighted = tensor * sine_table
    turned = jnp.concatenate([weighted[..., half_size:], -weighted[..., :half_size]], axis=-1)
    return tensor * cosine_table + turned


def block_scores(query_block, key_block, segment_query, segment_key, block_rows, scale):
    reach = WINDOW // 2
    scores = (
        jnp.einsum("qhd,khd->hqk", query_block, key_block, preferred_element_type=jnp.float32)
        * scale
    )
    offset = jnp.arange(block_rows)[:, None] + reach - jnp.arange(block_rows + 2 * reach)[None, :]
    valid = (jnp.abs(offset) <= reach) & (segment_query[:, None] == segment_key[None, :])
    return jnp.where(valid[None], scores, MASKED)


def band_pads(keys, values, segments):
    reach = WINDOW // 2
    pad_keys = jnp.pad(keys, ((reach, reach), (0, 0), (0, 0)))
    pad_values = jnp.pad(values, ((reach, reach), (0, 0), (0, 0)))
    pad_segments = jnp.pad(segments, (reach, reach), constant_values=-1)
    return (pad_keys, pad_values, pad_segments)


def band_forward(queries, keys, values, segments):
    length, heads, head_size = queries.shape
    reach = WINDOW // 2
    block = min(length, 512)
    scale = head_size ** (-0.5)
    pad_keys, pad_values, pad_segments = band_pads(keys, values, segments)

    def one_block(index):
        start = index * block
        query_block = lax.dynamic_slice_in_dim(queries, start, block, 0)
        key_block = lax.dynamic_slice_in_dim(pad_keys, start, block + 2 * reach, 0)
        value_block = lax.dynamic_slice_in_dim(pad_values, start, block + 2 * reach, 0)
        segment_query = lax.dynamic_slice_in_dim(segments, start, block, 0)
        segment_key = lax.dynamic_slice_in_dim(pad_segments, start, block + 2 * reach, 0)
        scores = block_scores(query_block, key_block, segment_query, segment_key, block, scale)
        peak = jnp.max(scores, axis=-1, keepdims=True)
        log_total = peak + jnp.log(jnp.sum(jnp.exp(scores - peak), axis=-1, keepdims=True))
        weights = jnp.exp(scores - log_total).astype(jnp.bfloat16)
        context = jnp.einsum(
            "hqk,khd->qhd", weights, value_block, preferred_element_type=jnp.float32
        ).astype(jnp.bfloat16)
        return (context, log_total[..., 0])

    contexts, totals = lax.map(one_block, jnp.arange(length // block, dtype=jnp.int32))
    return (contexts.reshape(length, heads, head_size), totals)


def band_backward(queries, keys, values, segments, grad_context, totals):
    length, heads, head_size = queries.shape
    reach = WINDOW // 2
    block = min(length, 512)
    span = block + 2 * reach
    scale = head_size ** (-0.5)
    pad_keys, pad_values, pad_segments = band_pads(keys, values, segments)

    def one_block(carry, index):
        grad_keys, grad_values = carry
        start = index * block
        query_block = lax.dynamic_slice_in_dim(queries, start, block, 0)
        key_block = lax.dynamic_slice_in_dim(pad_keys, start, span, 0)
        value_block = lax.dynamic_slice_in_dim(pad_values, start, span, 0)
        segment_query = lax.dynamic_slice_in_dim(segments, start, block, 0)
        segment_key = lax.dynamic_slice_in_dim(pad_segments, start, span, 0)
        grad_block = lax.dynamic_slice_in_dim(grad_context, start, block, 0)
        scores = block_scores(query_block, key_block, segment_query, segment_key, block, scale)
        probs = jnp.exp(scores - totals[index][..., None])
        grad_probs = jnp.einsum(
            "qhd,khd->hqk", grad_block, value_block, preferred_element_type=jnp.float32
        )
        delta = jnp.sum(probs * grad_probs, axis=-1, keepdims=True)
        grad_scores = (probs * (grad_probs - delta) * scale).astype(jnp.bfloat16)
        grad_query = jnp.einsum(
            "hqk,khd->qhd", grad_scores, key_block, preferred_element_type=jnp.float32
        )
        key_part = jnp.einsum(
            "hqk,qhd->khd", grad_scores, query_block, preferred_element_type=jnp.float32
        )
        value_part = jnp.einsum(
            "hqk,qhd->khd",
            probs.astype(jnp.bfloat16),
            grad_block,
            preferred_element_type=jnp.float32,
        )
        grad_keys = lax.dynamic_update_slice_in_dim(
            grad_keys, lax.dynamic_slice_in_dim(grad_keys, start, span, 0) + key_part, start, 0
        )
        grad_values = lax.dynamic_update_slice_in_dim(
            grad_values,
            lax.dynamic_slice_in_dim(grad_values, start, span, 0) + value_part,
            start,
            0,
        )
        return ((grad_keys, grad_values), grad_query)

    zeros = jnp.zeros((length + 2 * reach, heads, head_size), jnp.float32)
    (grad_keys, grad_values), grad_queries = lax.scan(
        one_block, (zeros, zeros), jnp.arange(length // block, dtype=jnp.int32)
    )
    return (
        grad_queries.reshape(length, heads, head_size),
        grad_keys[reach : reach + length],
        grad_values[reach : reach + length],
    )


def body(
    block_input,
    segment_ids,
    positions,
    attention_gain,
    feedforward_gain,
    qkv_weight,
    output_weight,
    expand_weight,
    contract_weight,
    cotangent,
):
    batches, local_rows, width = block_input.shape
    head_width = qkv_weight.shape[2]
    heads_here = head_width // HD
    unit_count = expand_weight.shape[2]
    qkv_full, expand_full, output_full, contract_full, first_gain, second_gain = (
        lax.all_gather(qkv_weight, "dp", axis=0, tiled=True),
        lax.all_gather(expand_weight, "dp", axis=0, tiled=True),
        lax.all_gather(output_weight, "dp", axis=1, tiled=True),
        lax.all_gather(contract_weight, "dp", axis=1, tiled=True),
        lax.all_gather(attention_gain, "dp", axis=0, tiled=True),
        lax.all_gather(feedforward_gain, "dp", axis=0, tiled=True),
    )
    qkv_matrix = qkv_full.reshape(width, 3 * head_width)
    expand_matrix = expand_full.reshape(width, 2 * unit_count)
    tokens = block_input[0]
    segments = segment_ids[0]
    cosine_table, sine_table = rope_tables(positions[0], HD)
    normed_one, inverse_one, rounded_one = layer_norm(tokens, first_gain)
    rows_one = lax.all_gather(rounded_one, "tensor", axis=0, tiled=True)
    length_all = rows_one.shape[0]
    projected = jnp.dot(rows_one, qkv_matrix, preferred_element_type=jnp.float32).reshape(
        length_all, 3, heads_here, HD
    )
    queries = rotate(projected[:, 0], cosine_table, sine_table).astype(jnp.bfloat16)
    keys = rotate(projected[:, 1], cosine_table, sine_table).astype(jnp.bfloat16)
    values_in = projected[:, 2].astype(jnp.bfloat16)
    context, totals = band_forward(queries, keys, values_in, segments)
    context_rows = context.reshape(length_all, head_width)
    attended = lax.psum_scatter(
        jnp.dot(context_rows, output_full, preferred_element_type=jnp.float32).astype(jnp.bfloat16),
        "tensor",
        scatter_dimension=0,
        tiled=True,
    ).astype(jnp.float32)
    residual = tokens + attended
    normed_two, inverse_two, rounded_two = layer_norm(residual, second_gain)
    rows_two = lax.all_gather(rounded_two, "tensor", axis=0, tiled=True)
    expanded = jnp.dot(rows_two, expand_matrix, preferred_element_type=jnp.float32).reshape(
        length_all, 2, unit_count
    )
    activated, slope = gelu_pair(expanded[:, 0])
    hidden = (activated * expanded[:, 1]).astype(jnp.bfloat16)
    contracted = lax.psum_scatter(
        jnp.dot(hidden, contract_full, preferred_element_type=jnp.float32).astype(jnp.bfloat16),
        "tensor",
        scatter_dimension=0,
        tiled=True,
    ).astype(jnp.float32)
    results = [residual + contracted]
    upstream = cotangent[0]
    rows_back = lax.all_gather(upstream.astype(jnp.bfloat16), "tensor", axis=0, tiled=True)
    grad_contract = jnp.dot(hidden.T, rows_back, preferred_element_type=jnp.float32)
    grad_hidden = jnp.dot(rows_back, contract_full.T, preferred_element_type=jnp.float32)
    grad_units = (
        jnp.stack([grad_hidden * expanded[:, 1] * slope, grad_hidden * activated], axis=1)
        .astype(jnp.bfloat16)
        .reshape(length_all, 2 * unit_count)
    )
    grad_expand = jnp.dot(rows_two.T, grad_units, preferred_element_type=jnp.float32)
    grad_two = lax.psum_scatter(
        jnp.dot(grad_units, expand_matrix.T, preferred_element_type=jnp.float32).astype(
            jnp.bfloat16
        ),
        "tensor",
        scatter_dimension=0,
        tiled=True,
    ).astype(jnp.float32)
    through_two, gain_part = norm_backward(grad_two, normed_two, inverse_two, second_gain)
    gain_second = gain_part
    grad_mid = upstream + through_two
    rows_mid = lax.all_gather(grad_mid.astype(jnp.bfloat16), "tensor", axis=0, tiled=True)
    grad_output = jnp.dot(context_rows.T, rows_mid, preferred_element_type=jnp.float32)
    grad_context = (
        jnp.dot(rows_mid, output_full.T, preferred_element_type=jnp.float32)
        .astype(jnp.bfloat16)
        .reshape(length_all, heads_here, HD)
    )
    grad_queries, grad_keys, grad_values = band_backward(
        queries, keys, values_in, segments, grad_context, totals
    )
    grad_proj = (
        jnp.stack(
            [
                unrotate(grad_queries, cosine_table, sine_table),
                unrotate(grad_keys, cosine_table, sine_table),
                grad_values,
            ],
            axis=1,
        )
        .astype(jnp.bfloat16)
        .reshape(length_all, 3 * head_width)
    )
    grad_qkv = jnp.dot(rows_one.T, grad_proj, preferred_element_type=jnp.float32)
    grad_one = lax.psum_scatter(
        jnp.dot(grad_proj, qkv_matrix.T, preferred_element_type=jnp.float32).astype(jnp.bfloat16),
        "tensor",
        scatter_dimension=0,
        tiled=True,
    ).astype(jnp.float32)
    through_one, gain_part = norm_backward(grad_one, normed_one, inverse_one, first_gain)
    input_grads = [grad_mid + through_one]
    gains_local = jnp.stack([gain_part, gain_second])
    owned_qkv, owned_expand, owned_output, owned_contract, owned_gains = (
        lax.psum_scatter(
            grad_qkv.reshape(width, 3, head_width).astype(jnp.bfloat16),
            "dp",
            scatter_dimension=0,
            tiled=True,
        ).astype(jnp.float32),
        lax.psum_scatter(
            grad_expand.reshape(width, 2, unit_count).astype(jnp.bfloat16),
            "dp",
            scatter_dimension=0,
            tiled=True,
        ).astype(jnp.float32),
        lax.psum_scatter(
            grad_output.astype(jnp.bfloat16), "dp", scatter_dimension=1, tiled=True
        ).astype(jnp.float32),
        lax.psum_scatter(
            grad_contract.astype(jnp.bfloat16), "dp", scatter_dimension=1, tiled=True
        ).astype(jnp.float32),
        lax.psum_scatter(
            gains_local.astype(jnp.bfloat16), "dp", scatter_dimension=1, tiled=True
        ).astype(jnp.float32),
    )
    gains_total = lax.psum(owned_gains, "tensor")
    return (
        jnp.stack(results),
        jnp.stack(input_grads),
        gains_total[0],
        gains_total[1],
        owned_qkv,
        owned_output,
        owned_expand,
        owned_contract,
    )


def solution(mesh):
    return jax.shard_map(
        body,
        mesh=mesh,
        in_specs=(
            P("dp", "tensor", None),
            P("dp", None),
            P("dp", None),
            P("dp"),
            P("dp"),
            P("dp", None, "tensor"),
            P("tensor", "dp"),
            P("dp", None, "tensor"),
            P("tensor", "dp"),
            P("dp", "tensor", None),
        ),
        out_specs=(
            P("dp", "tensor", None),
            P("dp", "tensor", None),
            P("dp"),
            P("dp"),
            P("dp", None, "tensor"),
            P("tensor", "dp"),
            P("dp", None, "tensor"),
            P("tensor", "dp"),
        ),
        check_vma=False,
    )
```

profile of v0, /device:TPU:0, one launch (start us, length us, event | category | flops | bytes accessed | tf_op | source)
XLA Modules:
  0.0 944.2 jit_solution(6730951717546695902)
XLA Ops:
  11.7 6.0 all-gather
  19.1 6.3 all_gather.33
  26.5 9.2 all_gather.32
  35.6 57.8 %all-gather.8.cloned.1.call-done = bf16[2048,1024]{1,0:T(8,128)(2,1)} async-done(((bf16[256,1024]{1,0:T(8,128)(2,1)}), bf16[2048,1024]{1,0:T(8,128)(2,1)}) %all-gather.8.cloned.1.call-update) | async-done | bytes 4194320 | tf_op jit(solution)/shard_map/all_gather | solution.py:196
  100.9 22.1 %while.26 = (s32[]{:T(128)}, bf16[4,512,2,64]{1,3,2,0:T(8,128)(2,1)S(1)}, f32[4,2,512]{2,1,0:T(2,128)S(1)}, s32[4]{0:T(128)S(1)}, bf16[2176,2,64]{0,2,1:T(8,128)...) while((s32[]{:T(128)}, ...), condition=%wide.region_5.6_spmd, body=%wide.region_2.5_spmd.sunk | while | flops 176684544 | bytes 9815796 | solution.py:104
  133.3 81.3 %reduce-scatter.12.cloned.1.call-done = bf16[256,1024]{1,0:T(8,128)(2,1)} async-done(((bf16[2048,1024]{1,0:T(8,128)(2,1)}), bf16[256,1024]{1,0:T(8,128)(2,1)}) %reduce-scatter.12.cloned.1.call-update) | async-done | bytes 524304 | tf_op jit(solution)/shard_map/reduce_scatter | solution.py:206
  219.4 8.4 all_gather.37
  227.8 61.6 %all-gather.10.cloned.1.call-done = bf16[2048,1024]{1,0:T(8,128)(2,1)} async-done(((bf16[256,1024]{1,0:T(8,128)(2,1)}), bf16[2048,1024]{1,0:T(8,128)(2,1)}) %all-gather.10.cloned.1.call-update) | async-done | bytes 4194320 | tf_op jit(solution)/shard_map/all_gather | solution.py:214
  289.5 7.9 fusion.74
  297.4 65.8 %all-gather.14.cloned.1.call-done = bf16[2048,1024]{1,0:T(8,128)(2,1)} async-done(((bf16[256,1024]{1,0:T(8,128)(2,1)}), bf16[2048,1024]{1,0:T(8,128)(2,1)}) %all-gather.14.cloned.1.call-update) | async-done | bytes 4194320 | tf_op jit(solution)/shard_map/all_gather | solution.py:228
  363.2 6.9 fusion.80
  385.3 78.5 %reduce-scatter.16.cloned.1.call-done = bf16[256,1024]{1,0:T(8,128)(2,1)} async-done(((bf16[2048,1024]{1,0:T(8,128)(2,1)}), bf16[256,1024]{1,0:T(8,128)(2,1)}) %reduce-scatter.16.cloned.1.call-update) | async-done | bytes 524304 | tf_op jit(solution)/shard_map/reduce_scatter | solution.py:237
  465.3 89.9 %reduce-scatter.14.cloned.1.call-done = bf16[256,1024]{1,0:T(8,128)(2,1)} async-done(((bf16[2048,1024]{1,0:T(8,128)(2,1)}), bf16[256,1024]{1,0:T(8,128)(2,1)}) %reduce-scatter.14.cloned.1.call-update) | async-done | bytes 524304 | tf_op jit(solution)/shard_map/reduce_scatter | solution.py:220
  563.9 7.0 fusion.83
  570.9 59.8 %all-gather.16.cloned.1.call-done = bf16[2048,1024]{1,0:T(8,128)(2,1)} async-done(((bf16[256,1024]{1,0:T(8,128)(2,1)}), bf16[2048,1024]{1,0:T(8,128)(2,1)}) %all-gather.16.cloned.1.call-update) | async-done | bytes 4194320 | tf_op jit(solution)/shard_map/all_gather | solution.py:248
  637.5 105.5 %while.27 = (s32[]{:T(128)}, f32[2176,2,64]{0,2,1:T(8,128)}, f32[2176,2,64]{0,2,1:T(8,128)}, f32[4,512,2,64]{1,0,3,2:T(4,128)}, s32[4]{0:T(128)S(1)}, /*index=5*...) while((s32[]{:T(128)}, f32[2176,2,64]{0,2,1:T(8,128)}, ...), condition=%wide.region_15.16_spmd, body=%wide.region_13.15_spmd.sunk | while | flops 430411520 | bytes 33158988 | solution.py:156
  651.5 6.1 dynamic_update_slice.31
  678.0 6.1 dynamic_update_slice.31
  704.4 6.1 dynamic_update_slice.31
  730.6 6.1 dynamic_update_slice.31
  776.0 24.1 %reduce-scatter.20.cloned.1.call-done = bf16[256,3,128]{2,0,1:T(8,128)(2,1)} async-done(((bf16[1024,3,128]{2,0,1:T(8,128)(2,1)}), bf16[256,3,128]{2,0,1:T(8,128)(2,1)}) %reduce-scatter.20.cloned.1.call-update) | async-done | bytes 196624 | tf_op jit(solution)/shard_map/reduce_scatter | solution.py:281
  801.8 90.0 %reduce-scatter.18.cloned.1.call-done = bf16[256,1024]{1,0:T(8,128)(2,1)} async-done(((bf16[2048,1024]{1,0:T(8,128)(2,1)}), bf16[256,1024]{1,0:T(8,128)(2,1)}) %reduce-scatter.18.cloned.1.call-update) | async-done | bytes 524304 | tf_op jit(solution)/shard_map/reduce_scatter | solution.py:271
  896.7 17.3 %reduce-scatter.28.cloned.1.call-done = bf16[256,2]{1,0:T(8,128)(2,1)} async-done(((bf16[1024,2]{1,0:T(8,128)(2,1)}), bf16[256,2]{1,0:T(8,128)(2,1)}) %reduce-scatter.28.cloned.1.call-update) | async-done | bytes 1040
  914.9 21.4 %psum.7 = f32[2,256]{1,0:T(2,128)S(1)} all-reduce(bf16[2,256]{1,0:T(2,128)(2,1)S(1)} %copy.35), channel_id=1, replica_groups=mesh['dp'=4,'tensor'=8] {'tensor'}, use_global_device_ids=true, to_apply=%region_22.23 | all-reduce | flops 512 | bytes 3072 | tf_op jit(solution)/shard_map/psum | solution.py:303
  (242 shorter events, 191.1 us)
Async XLA Ops:
  8.0 9.7 %copy-start = (f32[1,256,1024]{2,1,0:T(8,128)S(1)}, f32[1,256,1024]{2,1,0:T(8,128)}, u32[]{:S(2)}) copy-start(f32[1,256,1024]{2,1,0:T(8,128)} %param.14) | copy-start | bytes 3145732
  8.0 10.8 %copy-start.15 = (bf16[256,3,128]{2,0,1:T(8,128)(2,1)S(1)}, bf16[256,3,128]{2,0,1:T(8,128)(2,1)}, u32[]{:S(2)}) copy-start(bf16[256,3,128]{2,0,1:T(8,128)(2,1)} %param.19) | copy-start | bytes 589828
  8.0 11.0 %copy-start.19 = (s32[1,2048]{1,0:T(1,128)S(1)}, s32[1,2048]{1,0:T(1,128)}, u32[]{:S(2)}) copy-start(s32[1,2048]{1,0:T(1,128)} %param.16) | copy-start | bytes 24580
  8.0 11.0 %copy-start.17 = (s32[1,2048]{1,0:T(1,128)S(1)}, s32[1,2048]{1,0:T(1,128)}, u32[]{:S(2)}) copy-start(s32[1,2048]{1,0:T(1,128)} %param.15) | copy-start | bytes 24580
  8.0 11.1 %copy-start.18 = (bf16[128,256]{1,0:T(8,128)(2,1)S(1)}, bf16[128,256]{1,0:T(8,128)(2,1)}, u32[]{:S(2)}) copy-start(bf16[128,256]{1,0:T(8,128)(2,1)} %param.20) | copy-start | bytes 196612
  8.1 85.4 %all-gather.8.cloned.1.call-start = ((), (), s32[]{:S(2)}) async-start(), calls=%async_computation.9 | async-start | bytes 4718592 | tf_op jit(solution)/shard_map/all_gather | solution.py:196
  18.8 195.9 %reduce-scatter.12.cloned.1.call-start = ((), (), s32[]{:S(2)}) async-start(), calls=%async_computation.10 | async-start | bytes 4718592 | tf_op jit(solution)/shard_map/reduce_scatter | solution.py:206
  26.5 71.7 %copy-start.4 = (f32[2048,64]{0,1:T(8,128)}, f32[2048,64]{0,1:T(8,128)S(1)}, u32[]{:S(2)}) copy-start(f32[2048,64]{0,1:T(8,128)S(1)} %get-tuple-element.205) | copy-start | bytes 1572868
  127.6 100.2 %all-gather.12.cloned.1.call-start = ((), (), s32[]{:S(2)}) async-start(), calls=%async_computation.12 | async-start | bytes 1679360 | tf_op jit(solution)/shard_map/all_gather | solution.py:184
  128.2 161.3 %all-gather.10.cloned.1.call-start = ((), (), s32[]{:S(2)}) async-start(), calls=%async_computation.11 | async-start | bytes 4718592 | tf_op jit(solution)/shard_map/all_gather | solution.py:214
  217.2 146.0 %all-gather.14.cloned.1.call-start = ((), (), s32[]{:S(2)}) async-start(), calls=%async_computation.14 | async-start | bytes 4718592 | tf_op jit(solution)/shard_map/all_gather | solution.py:228
  219.3 244.4 %reduce-scatter.16.cloned.1.call-start = ((), (), s32[]{:S(2)}) async-start(), calls=%async_computation.15 | async-start | bytes 4718592 | tf_op jit(solution)/shard_map/reduce_scatter | solution.py:237
  363.2 8.4 copy-start.21
  376.7 178.5 %reduce-scatter.14.cloned.1.call-start = ((), (), s32[]{:S(2)}) async-start(), calls=%async_computation.13 | async-start | bytes 4718592 | tf_op jit(solution)/shard_map/reduce_scatter | solution.py:220
  385.3 170.0 %copy-start.8 = (f32[1,256,1024]{2,1,0:T(8,128)S(1)}, f32[1,256,1024]{2,1,0:T(8,128)}, u32[]{:S(2)}) copy-start(f32[1,256,1024]{2,1,0:T(8,128)} %param.23) | copy-start | bytes 3145732
  385.3 245.5 %all-gather.16.cloned.1.call-start = ((), (), s32[]{:S(2)}) async-start(), calls=%async_computation.16 | async-start | bytes 4718592 | tf_op jit(solution)/shard_map/all_gather | solution.py:248
  558.5 209.8 %reduce-scatter.26.cloned.1.call-start = ((), (), s32[]{:S(2)}) async-start(), calls=%async_computation.21 | async-start | bytes 839680 | tf_op jit(solution)/shard_map/reduce_scatter | solution.py:296
  563.6 206.4 %reduce-scatter.24.cloned.1.call-start = ((), (), s32[]{:S(2)}) async-start(), calls=%async_computation.20 | async-start | bytes 1679360 | tf_op jit(solution)/shard_map/reduce_scatter | solution.py:287
  570.9 203.6 %reduce-scatter.22.cloned.1.call-start = ((), (), s32[]{:S(2)}) async-start(), calls=%async_computation.19 | async-start | bytes 327680 | tf_op jit(solution)/shard_map/reduce_scatter | solution.py:293
  755.9 44.1 %reduce-scatter.20.cloned.1.call-start = ((), (), s32[]{:S(2)}) async-start(), calls=%async_computation.18 | async-start | bytes 983040 | tf_op jit(solution)/shard_map/reduce_scatter | solution.py:281
  762.3 129.5 %reduce-scatter.18.cloned.1.call-start = ((), (), s32[]{:S(2)}) async-start(), calls=%async_computation.17 | async-start | bytes 4718592 | tf_op jit(solution)/shard_map/reduce_scatter | solution.py:271
  768.1 123.7 %copy-start.1 = (f32[1,256,1024]{2,1,0:T(8,128)S(1)}, f32[1,256,1024]{2,1,0:T(8,128)}, u32[]{:S(2)}) copy-start(f32[1,256,1024]{2,1,0:T(8,128)} %param.14) | copy-start | bytes 3145732
  768.2 126.1 %copy-start.6 = (f32[256,1024]{1,0:T(8,128)S(1)}, f32[256,1024]{1,0:T(8,128)}, u32[]{:S(2)}) copy-start(f32[256,1024]{1,0:T(8,128)} %get-tuple-element.176) | copy-start | bytes 3145732
  768.2 145.8 %reduce-scatter.28.cloned.1.call-start = ((), (), s32[]{:S(2)}) async-start(), calls=%async_computation.22 | async-start | bytes 327680
  (16 other events, 41.8 us)
Sparse Core Ops, SparseCore 0:
  18.9 74.5 all-gather.7
  127.7 86.8 reduce-scatter.11
  376.9 86.8 reduce-scatter.15
  467.3 87.9 reduce-scatter.13
Sparse Core Ops, SparseCore 1:
  129.6 16.9 all-gather.11
  217.3 72.1 all-gather.9
  292.0 71.1 all-gather.13
  558.5 72.2 all-gather.15
  633.9 21.1 reduce-scatter.25
  657.6 26.5 reduce-scatter.23
  756.0 18.4 reduce-scatter.21
  776.9 23.1 reduce-scatter.19
  803.6 88.2 reduce-scatter.17
  894.4 19.6 reduce-scatter.27
where the time goes:
time: 954 us; the launch traced here: 944 us
  waiting for transfers between devices  630 us (66%)
  matrix products  133 us (14%)
  blocking collectives  56.3 us (6%)
  local copies, waits for them, and re-layouts  52.7 us (6%)
  other arithmetic  42.4 us (4%)
  between operations  16.1 us (2%)
  loops' own time  13.3 us (1%)
    reduce_scatter x1, waiting for transfers between devices, body(): lax.psum_scatter(jnp.dot(grad_proj, qkv_matrix.T, preferred_element_type=...  90 us
    reduce_scatter x1, waiting for transfers between devices, body(): lax.psum_scatter(jnp.dot(hidden, contract_full, preferred_element_type=jn...  89.9 us
    reduce_scatter x1, waiting for transfers between devices, body(): lax.psum_scatter(jnp.dot(context_rows, output_full, preferred_element_typ...  81.3 us
    reduce_scatter x1, waiting for transfers between devices, body(): lax.psum_scatter(jnp.dot(grad_units, expand_matrix.T, preferred_element_t...  78.5 us
    all_gather x1, waiting for transfers between devices, body(): lax.all_gather(upstream.astype(jnp.bfloat16), 'tensor', axis=0, tiled=True)  65.8 us
    all_gather x1, waiting for transfers between devices, body(): rows_two = lax.all_gather(rounded_two, 'tensor', axis=0, tiled=True)  61.6 us
    all_gather x1, waiting for transfers between devices, body(): lax.all_gather(grad_mid.astype(jnp.bfloat16), 'tensor', axis=0, tiled=True)  59.8 us
    all_gather x1, waiting for transfers between devices, body(): rows_one = lax.all_gather(rounded_one, 'tensor', axis=0, tiled=True)  57.8 us
  transfers between devices with their start and end apart: 14, of which 11 were waited for; matrix products, arithmetic and copies ran while one was open for 18% of the time, Pallas kernels for 0%

commit v1 on v0

--- a/solution.py
+++ b/solution.py
@@ -245,7 +245,15 @@
     through_two, gain_part = norm_backward(grad_two, normed_two, inverse_two, second_gain)
     gain_second = gain_part
     grad_mid = upstream + through_two
-    rows_mid = lax.all_gather(grad_mid.astype(jnp.bfloat16), "tensor", axis=0, tiled=True)
+    array = grad_mid.astype(jnp.bfloat16)
+    ways, here = (lax.axis_size("tensor"), lax.axis_index("tensor"))
+    rows_mid, reach_2 = (array, 1)
+    while reach_2 < ways:
+        theirs = lax.ppermute(rows_mid, "tensor", [(d, d ^ reach_2) for d in range(ways)])
+        mine_first = jnp.concatenate([rows_mid, theirs], axis=0)
+        theirs_first = jnp.concatenate([theirs, rows_mid], axis=0)
+        rows_mid = jnp.where(here & reach_2 == 0, mine_first, theirs_first)
+        reach_2 = 2 * reach_2
     grad_output = jnp.dot(context_rows.T, rows_mid, preferred_element_type=jnp.float32)
     grad_context = (
         jnp.dot(rows_mid, output_full.T, preferred_element_type=jnp.float32)

time: 954 us -> 1020 us (1.069)
  waiting for transfers between devices: 630 us -> 671 us
    ppermute x0 -> x3, waiting for transfers between devices: none -> 111 us  [body(): lax.ppermute(rows_mid, 'tensor', [(d, d ^ reach_2) for d in range(ways)])]
    all_gather x1 -> x0, waiting for transfers between devices: 59.8 us -> none  [body(): lax.all_gather(grad_mid.astype(jnp.bfloat16), 'tensor', axis=0, tiled=True)]
    all_gather x1, blocking collectives: 8.41 us -> 19.1 us  [body(): lax.all_gather(contract_weight, 'dp', axis=1, tiled=True)]
    all_gather x1, waiting for transfers between devices: 61.6 us -> 51 us  [body(): rows_two = lax.all_gather(rounded_two, 'tensor', axis=0, tiled=True)]
  transfers between devices with their start and end apart: 14 -> 16, of which waited for: 11 -> 13; matrix products, arithmetic and copies ran while one was open for 18% -> 17% of each run, Pallas kernels for 0% -> 0%
where the time goes in v1:
time: 1020 us; the launch traced here: 1010 us
  waiting for transfers between devices  671 us (66%)
  matrix products  137 us (13%)
  blocking collectives  66.4 us (7%)
  local copies, waits for them, and re-layouts  55.7 us (5%)
  other arithmetic  46.6 us (5%)
  between operations  16.6 us (2%)
  loops' own time  13.2 us (1%)
    ppermute x3, waiting for transfers between devices, body(): lax.ppermute(rows_mid, 'tensor', [(d, d ^ reach_2) for d in range(ways)])  111 us
    reduce_scatter x1, waiting for transfers between devices, body(): lax.psum_scatter(jnp.dot(grad_proj, qkv_matrix.T, preferred_element_type=...  90 us
    reduce_scatter x1, waiting for transfers between devices, body(): lax.psum_scatter(jnp.dot(hidden, contract_full, preferred_element_type=jn...  89.9 us
    reduce_scatter x1, waiting for transfers between devices, body(): lax.psum_scatter(jnp.dot(context_rows, output_full, preferred_element_typ...  81.3 us
    reduce_scatter x1, waiting for transfers between devices, body(): lax.psum_scatter(jnp.dot(grad_units, expand_matrix.T, preferred_element_t...  78.4 us
    all_gather x1, waiting for transfers between devices, body(): lax.all_gather(upstream.astype(jnp.bfloat16), 'tensor', axis=0, tiled=True)  65.8 us
    all_gather x1, waiting for transfers between devices, body(): rows_one = lax.all_gather(rounded_one, 'tensor', axis=0, tiled=True)  58.3 us
    all_gather x1, waiting for transfers between devices, body(): rows_two = lax.all_gather(rounded_two, 'tensor', axis=0, tiled=True)  51 us
  transfers between devices with their start and end apart: 16, of which 13 were waited for; matrix products, arithmetic and copies ran while one was open for 17% of the time, Pallas kernels for 0%

profile of v1, /device:TPU:0, one launch (start us, length us, event | category | flops | bytes accessed | tf_op | source)
XLA Modules:
  0.0 1013.9 jit_solution(69204000788837644)
XLA Ops:
  19.1 6.3 all_gather.30
  26.5 8.7 all_gather.29
  35.2 58.3 %all-gather.7.cloned.1.call-done = bf16[2048,1024]{1,0:T(8,128)(2,1)} async-done(((bf16[256,1024]{1,0:T(8,128)(2,1)}), bf16[2048,1024]{1,0:T(8,128)(2,1)}) %all-gather.7.cloned.1.call-update) | async-done | bytes 4194320 | tf_op jit(solution)/shard_map/all_gather | solution.py:196
  99.8 24.3 %while.26 = (s32[]{:T(128)}, bf16[4,512,2,64]{1,3,2,0:T(8,128)(2,1)}, f32[4,2,512]{2,1,0:T(2,128)S(1)}, s32[4]{0:T(128)S(1)}, bf16[2176,2,64]{0,2,1:T(8,128)(2,1...) while((s32[]{:T(128)}, ...), condition=%wide.region_5.6_spmd, body=%wide.region_2.5_spmd.sunk | while | flops 176684544 | bytes 9816304 | solution.py:104
  135.9 81.3 %reduce-scatter.12.cloned.1.call-done = bf16[256,1024]{1,0:T(8,128)(2,1)} async-done(((bf16[2048,1024]{1,0:T(8,128)(2,1)}), bf16[256,1024]{1,0:T(8,128)(2,1)}) %reduce-scatter.12.cloned.1.call-update) | async-done | bytes 524304 | tf_op jit(solution)/shard_map/reduce_scatter | solution.py:206
  221.9 19.1 %all_gather.34 = bf16[328,1024]{1,0:T(8,128)(2,1)S(1)} all-gather(bf16[328,256]{1,0:T(8,128)(2,1)S(1)} %copy-done.19), channel_id=1, replica_groups=mesh['dp'=4,'tensor'=8] {'dp'}, dimensions={1}, use_global_device_ids=true | all-gather | bytes 839680 | tf_op jit(solution)/shard_map/all_gather | solution.py:186
  241.0 51.0 %all-gather.9.cloned.1.call-done = bf16[2048,1024]{1,0:T(8,128)(2,1)} async-done(((bf16[256,1024]{1,0:T(8,128)(2,1)}), bf16[2048,1024]{1,0:T(8,128)(2,1)}) %all-gather.9.cloned.1.call-update) | async-done | bytes 4194320 | tf_op jit(solution)/shard_map/all_gather | solution.py:214
  292.0 8.0 fusion.74
  299.9 65.8 %all-gather.13.cloned.1.call-done = bf16[2048,1024]{1,0:T(8,128)(2,1)} async-done(((bf16[256,1024]{1,0:T(8,128)(2,1)}), bf16[2048,1024]{1,0:T(8,128)(2,1)}) %all-gather.13.cloned.1.call-update) | async-done | bytes 4194320 | tf_op jit(solution)/shard_map/all_gather | solution.py:228
  365.7 6.9 fusion.80
  387.9 78.4 %reduce-scatter.16.cloned.1.call-done = bf16[256,1024]{1,0:T(8,128)(2,1)} async-done(((bf16[2048,1024]{1,0:T(8,128)(2,1)}), bf16[256,1024]{1,0:T(8,128)(2,1)}) %reduce-scatter.16.cloned.1.call-update) | async-done | bytes 524304 | tf_op jit(solution)/shard_map/reduce_scatter | solution.py:237
  467.9 89.9 %reduce-scatter.14.cloned.1.call-done = bf16[256,1024]{1,0:T(8,128)(2,1)} async-done(((bf16[2048,1024]{1,0:T(8,128)(2,1)}), bf16[256,1024]{1,0:T(8,128)(2,1)}) %reduce-scatter.14.cloned.1.call-update) | async-done | bytes 524304 | tf_op jit(solution)/shard_map/reduce_scatter | solution.py:220
  562.1 11.8 %collective-permute-done = bf16[256,1024]{1,0:T(8,128)(2,1)S(1)} collective-permute-done((bf16[256,1024]{1,0:T(8,128)(2,1)S(1)}, bf16[256,1024]{1,0:T(8,128)(2,1)S(1)}, u32[]{:S(2)}, u32[]{:S(2)}) %collective-permute-start) | collective-permute-done | bytes 524320 | tf_op jit(solution)/shard_map/ppermute | solution.py:252
  576.2 22.1 %collective-permute-done.1 = bf16[512,1024]{1,0:T(8,128)(2,1)} collective-permute-done((bf16[512,1024]{1,0:T(8,128)(2,1)S(1)}, bf16[512,1024]{1,0:T(8,128)(2,1)}, u32[]{:S(2)}, u32[]{:S(2)}) %collective-permute-start.1) | collective-permute-done | bytes 1048608 | tf_op jit(solution)/shard_map/ppermute | solution.py:252
  609.6 7.0 fusion.83
  616.8 77.2 %collective-permute-done.2 = bf16[1024,1024]{1,0:T(8,128)(2,1)} collective-permute-done((bf16[1024,1024]{1,0:T(8,128)(2,1)}, bf16[1024,1024]{1,0:T(8,128)(2,1)}, u32[]{:S(2)}, u32[]{:S(2)}) %collective-permute-start.2) | collective-permute-done | bytes 2097184 | tf_op jit(solution)/shard_map/ppermute | solution.py:252
  701.6 105.4 %while.27 = (s32[]{:T(128)}, f32[2176,2,64]{0,2,1:T(8,128)}, f32[2176,2,64]{0,2,1:T(8,128)}, f32[4,512,2,64]{1,0,3,2:T(4,128)}, s32[4]{0:T(128)S(1)}, /*index=5*...) while((s32[]{:T(128)}, f32[2176,2,64]{0,2,1:T(8,128)}, ...), condition=%wide.region_15.16_spmd, body=%wide.region_13.15_spmd.sunk | while | flops 430411520 | bytes 33158988 | solution.py:156
  715.6 6.1 dynamic_update_slice.31
  741.9 6.1 dynamic_update_slice.31
  768.3 6.1 dynamic_update_slice.31
  845.3 24.1 %reduce-scatter.20.cloned.1.call-done = bf16[256,3,128]{2,0,1:T(8,128)(2,1)} async-done(((bf16[1024,3,128]{2,0,1:T(8,128)(2,1)}), bf16[256,3,128]{2,0,1:T(8,128)(2,1)}) %reduce-scatter.20.cloned.1.call-update) | async-done | bytes 196624 | tf_op jit(solution)/shard_map/reduce_scatter | solution.py:289
  871.1 90.0 %reduce-scatter.18.cloned.1.call-done = bf16[256,1024]{1,0:T(8,128)(2,1)} async-done(((bf16[2048,1024]{1,0:T(8,128)(2,1)}), bf16[256,1024]{1,0:T(8,128)(2,1)}) %reduce-scatter.18.cloned.1.call-update) | async-done | bytes 524304 | tf_op jit(solution)/shard_map/reduce_scatter | solution.py:279
  966.0 17.3 %reduce-scatter.28.cloned.1.call-done = bf16[256,2]{1,0:T(8,128)(2,1)} async-done(((bf16[1024,2]{1,0:T(8,128)(2,1)}), bf16[256,2]{1,0:T(8,128)(2,1)}) %reduce-scatter.28.cloned.1.call-update) | async-done | bytes 1040
  984.2 21.3 %psum.7 = f32[2,256]{1,0:T(2,128)S(1)} all-reduce(bf16[2,256]{1,0:T(2,128)(2,1)S(1)} %copy.35), channel_id=1, replica_groups=mesh['dp'=4,'tensor'=8] {'tensor'}, use_global_device_ids=true, to_apply=%region_22.23 | all-reduce | flops 512 | bytes 3072 | tf_op jit(solution)/shard_map/psum | solution.py:311
  (251 shorter events, 221.4 us)
Async XLA Ops:
  8.0 11.0 %copy-start.20 = (s32[1,2048]{1,0:T(1,128)S(1)}, s32[1,2048]{1,0:T(1,128)}, u32[]{:S(2)}) copy-start(s32[1,2048]{1,0:T(1,128)} %param.15) | copy-start | bytes 24580
  8.0 11.1 %copy-start.21 = (bf16[128,256]{1,0:T(8,128)(2,1)S(1)}, bf16[128,256]{1,0:T(8,128)(2,1)}, u32[]{:S(2)}) copy-start(bf16[128,256]{1,0:T(8,128)(2,1)} %param.20) | copy-start | bytes 196612
  8.1 85.4 %all-gather.7.cloned.1.call-start = ((), (), s32[]{:S(2)}) async-start(), calls=%async_computation.9 | async-start | bytes 4718592 | tf_op jit(solution)/shard_map/all_gather | solution.py:196
  18.8 198.4 %reduce-scatter.12.cloned.1.call-start = ((), (), s32[]{:S(2)}) async-start(), calls=%async_computation.10 | async-start | bytes 4718592 | tf_op jit(solution)/shard_map/reduce_scatter | solution.py:206
  26.5 71.5 %copy-start.3 = (f32[2048,64]{0,1:T(8,128)}, f32[2048,64]{0,1:T(8,128)S(1)}, u32[]{:S(2)}) copy-start(f32[2048,64]{0,1:T(8,128)S(1)} %get-tuple-element.205) | copy-start | bytes 1572868
  35.2 62.3 %copy-start.15 = (bf16[1024,3,128]{0,2,1:T(8,128)(2,1)}, bf16[1024,3,128]{0,2,1:T(8,128)(2,1)S(1)}, u32[]{:S(2)}) copy-start(bf16[1024,3,128]{0,2,1:T(8,128)(2,1)S(1)} %all_gather.29) | copy-start | bytes 2359300
  130.1 110.8 %all-gather.11.cloned.1.call-start = ((), (), s32[]{:S(2)}) async-start(), calls=%async_computation.12 | async-start | bytes 1679360 | tf_op jit(solution)/shard_map/all_gather | solution.py:184
  130.7 161.2 %all-gather.9.cloned.1.call-start = ((), (), s32[]{:S(2)}) async-start(), calls=%async_computation.11 | async-start | bytes 4718592 | tf_op jit(solution)/shard_map/all_gather | solution.py:214
  219.7 146.0 %all-gather.13.cloned.1.call-start = ((), (), s32[]{:S(2)}) async-start(), calls=%async_computation.14 | async-start | bytes 4718592 | tf_op jit(solution)/shard_map/all_gather | solution.py:228
  221.8 244.5 %reduce-scatter.16.cloned.1.call-start = ((), (), s32[]{:S(2)}) async-start(), calls=%async_computation.15 | async-start | bytes 4718592 | tf_op jit(solution)/shard_map/reduce_scatter | solution.py:237
  379.3 178.5 %reduce-scatter.14.cloned.1.call-start = ((), (), s32[]{:S(2)}) async-start(), calls=%async_computation.13 | async-start | bytes 4718592 | tf_op jit(solution)/shard_map/reduce_scatter | solution.py:220
  387.8 170.0 %copy-start.8 = (f32[1,256,1024]{2,1,0:T(8,128)S(1)}, f32[1,256,1024]{2,1,0:T(8,128)}, u32[]{:S(2)}) copy-start(f32[1,256,1024]{2,1,0:T(8,128)} %param.23) | copy-start | bytes 3145732
  387.8 448.7 %reduce-scatter.26.cloned.1.call-start = ((), (), s32[]{:S(2)}) async-start(), calls=%async_computation.20 | async-start | bytes 839680 | tf_op jit(solution)/shard_map/reduce_scatter | solution.py:304
  560.6 13.3 %collective-permute-start = (bf16[256,1024]{1,0:T(8,128)(2,1)S(1)}, bf16[256,1024]{1,0:T(8,128)(2,1)S(1)}, u32[]{:S(2)}, u32[]{:S(2)}) collective-permute-start(bf16[256,1024]{1,0:T(8,128)(2,1)S(1)} %get-tuple-element.175), channel_id=1, source_target_pairs={{0,1},{1,0},{2,3},{3,2},{4,5},{5,4},{6,7},{7,6},{8,9},{9,8},{10,11... | collective-permute-start | bytes 1572872 | tf_op jit(solution)/shard_map/ppermute | solution.py:252
  574.4 30.5 %copy-start.14 = (bf16[2048,328]{0,1:T(8,128)(2,1)S(1)}, bf16[2048,328]{0,1:T(8,128)(2,1)}, u32[]{:S(2)}) copy-start(bf16[2048,328]{0,1:T(8,128)(2,1)} %copy-done.13) | copy-start | bytes 4030468
  574.4 23.8 %collective-permute-start.1 = (bf16[512,1024]{1,0:T(8,128)(2,1)S(1)}, bf16[512,1024]{1,0:T(8,128)(2,1)}, u32[]{:S(2)}, u32[]{:S(2)}) collective-permute-start(bf16[512,1024]{1,0:T(8,128)(2,1)S(1)} %maximum_select_fusion.2), channel_id=1, source_target_pairs={{0,2},{1,3},{2,0},{3,1},{4,6},{5,7},{6,4},{7,5},{8,10},{9,11},{10,... | collective-permute-start | bytes 3145736 | tf_op jit(solution)/shard_map/ppermute | solution.py:252
  602.2 91.8 %collective-permute-start.2 = (bf16[1024,1024]{1,0:T(8,128)(2,1)}, bf16[1024,1024]{1,0:T(8,128)(2,1)}, u32[]{:S(2)}, u32[]{:S(2)}) collective-permute-start(bf16[1024,1024]{1,0:T(8,128)(2,1)} %maximum_select_fusion.1), channel_id=1, source_target_pairs={{0,4},{1,5},{2,6},{3,7},{4,0},{5,1},{6,2},{7,3},{8,12},{9,13},{10,... | collective-permute-start | bytes 6291464 | tf_op jit(solution)/shard_map/ppermute | solution.py:252
  609.5 228.8 %reduce-scatter.24.cloned.1.call-start = ((), (), s32[]{:S(2)}) async-start(), calls=%async_computation.19 | async-start | bytes 1679360 | tf_op jit(solution)/shard_map/reduce_scatter | solution.py:295
  616.6 227.1 %reduce-scatter.22.cloned.1.call-start = ((), (), s32[]{:S(2)}) async-start(), calls=%async_computation.18 | async-start | bytes 327680 | tf_op jit(solution)/shard_map/reduce_scatter | solution.py:301
  822.6 46.8 %reduce-scatter.20.cloned.1.call-start = ((), (), s32[]{:S(2)}) async-start(), calls=%async_computation.17 | async-start | bytes 983040 | tf_op jit(solution)/shard_map/reduce_scatter | solution.py:289
  830.3 130.7 %reduce-scatter.18.cloned.1.call-start = ((), (), s32[]{:S(2)}) async-start(), calls=%async_computation.16 | async-start | bytes 4718592 | tf_op jit(solution)/shard_map/reduce_scatter | solution.py:279
  836.4 124.6 %copy-start.1 = (f32[1,256,1024]{2,1,0:T(8,128)S(1)}, f32[1,256,1024]{2,1,0:T(8,128)}, u32[]{:S(2)}) copy-start(f32[1,256,1024]{2,1,0:T(8,128)} %param.14) | copy-start | bytes 3145732
  836.5 127.1 %copy-start.7 = (f32[256,1024]{1,0:T(8,128)S(1)}, f32[256,1024]{1,0:T(8,128)}, u32[]{:S(2)}) copy-start(f32[256,1024]{1,0:T(8,128)} %get-tuple-element.176) | copy-start | bytes 3145732
  836.5 146.8 %reduce-scatter.28.cloned.1.call-start = ((), (), s32[]{:S(2)}) async-start(), calls=%async_computation.21 | async-start | bytes 327680
  (20 other events, 85.1 us)
Sparse Core Ops, SparseCore 0:
  18.9 74.5 all-gather.6
  130.2 86.8 reduce-scatter.11
  379.4 86.8 reduce-scatter.15
  469.8 87.9 reduce-scatter.13
Sparse Core Ops, SparseCore 1:
  132.2 16.9 all-gather.10
  219.8 72.1 all-gather.8
  294.5 71.1 all-gather.12
  609.6 21.3 reduce-scatter.25
  633.6 26.6 reduce-scatter.23
  822.7 21.0 reduce-scatter.21
  846.2 23.1 reduce-scatter.19
  872.8 88.2 reduce-scatter.17
  963.6 19.6 reduce-scatter.27
